TPU v7x, 128 devices: a whole 4x4x4 slice. The times are simulated.
128 devices in a mesh: section: 2 (over x_lo), dp: 16 (over x_hi, y, core), mp: 4 (over z).
Axes of the slice: x: 4 (x_hi: 2, x_lo: 2; x = x_hi * 2 + x_lo), y: 4, z: 4, core: 2. Of those that a mesh axis runs over, the one named last changes fastest.
Arguments:
- hidden: bfloat16 [2, 16, 256, 5120], P('section', 'dp'), may hold values from -6 to 6
- gain: float32 [2, 5120], P('section'), may hold values from 0.5 to 2
- w_first: bfloat16 [2, 5120, 2560], P('section', 'dp', 'mp'), may hold values from -0.078125 to 0.078125
- w_second: bfloat16 [2, 5120, 2560], P('section', 'dp', 'mp'), may hold values from -0.078125 to 0.078125
- lengths: int32 [16, 2], P('dp'), may hold values from 32 to 256, as said below
- cotangent: bfloat16 [2, 16, 256, 5120], P('section', 'dp'), may hold values from -6 to 6
Outputs:
- result: bfloat16 [2, 16, 256, 5120], P('section', 'dp')
- d_hidden: bfloat16 [2, 16, 256, 5120], P('section', 'dp')
- d_gain: float32 [2, 5120], P('section', 'dp')
- d_first: float32 [2, 5120, 2560], P('section', 'dp', 'mp')
- d_second: float32 [2, 5120, 2560], P('section', 'dp', 'mp')
Inputs may be any that keep to these rules, and one draw needn't show every extreme that they name: `lengths`: each row's source count and target count; positions at or past a count are padding.
All inputs are finite; a program needn't handle non-finite values.
Results may differ from a plain program's by a relative error of at most 0.017.
Values may be sent and summed in bfloat16 or wider, within the bound.
A program may use at most 128 MiB of HBM per device.

v0:
```python
import math
import jax
import jax.numpy as jnp
from jax import lax
from jax.sharding import PartitionSpec as P

HEAD = 128
EPS = 1e-06
MASKED = -1e30


def passed_along(shard, axis, by):
    peers = lax.axis_size(axis)
    pairs = [(i, i + by) for i in range(peers) if 0 <= i + by < peers]
    return lax.ppermute(shard, axis, pairs)


def contract_rows(left, right):
    return lax.dot_general(
        left, right, (((0,), (0,)), ((), ())), preferred_element_type=jnp.float32
    )


def contract_last(left, right):
    return lax.dot_general(
        left, right, (((1,), (1,)), ((), ())), preferred_element_type=jnp.float32
    )


def total_features(partial_value):
    return lax.psum(partial_value, "mp")


def split_heads(values_in):
    batch_size, length, columns = values_in.shape
    return values_in.reshape(batch_size, length, columns // HEAD, HEAD)


def attend(queries, keys, values, key_count):
    batch_size, length, columns = queries.shape
    scale = 1.0 / math.sqrt(HEAD)
    scores = (
        jnp.einsum(
            "bqhd,bkhd->bhqk",
            split_heads(queries),
            split_heads(keys),
            preferred_element_type=jnp.float32,
        )
        * scale
    )
    visible = jnp.arange(length)[None, None, None, :] < key_count[:, None, None, None]
    scores = jnp.where(visible, scores, MASKED)
    weights = jax.nn.softmax(scores, axis=-1)
    weights_low = weights.astype(jnp.bfloat16)
    context = jnp.einsum(
        "bhqk,bkhd->bqhd", weights_low, split_heads(values), preferred_element_type=jnp.float32
    )
    return (context.reshape(batch_size, length, columns).astype(jnp.bfloat16), weights, weights_low)


def attend_back(grad_context, queries, keys, values, weights, weights_low):
    batch_size, length, columns = queries.shape
    scale = 1.0 / math.sqrt(HEAD)
    grad_heads = split_heads(grad_context)
    grad_weights = jnp.einsum(
        "bqhd,bkhd->bhqk", grad_heads, split_heads(values), preferred_element_type=jnp.float32
    )
    grad_values = jnp.einsum(
        "bhqk,bqhd->bkhd", weights_low, grad_heads, preferred_element_type=jnp.float32
    )
    centered = grad_weights - jnp.sum(weights * grad_weights, axis=-1, keepdims=True)
    grad_scores = (weights * centered * scale).astype(jnp.bfloat16)
    grad_queries = jnp.einsum(
        "bhqk,bkhd->bqhd", grad_scores, split_heads(keys), preferred_element_type=jnp.float32
    )
    grad_keys = jnp.einsum(
        "bhqk,bqhd->bkhd", grad_scores, split_heads(queries), preferred_element_type=jnp.float32
    )
    shape_out = (batch_size, length, columns)
    return (
        grad_queries.reshape(shape_out).astype(jnp.bfloat16),
        grad_keys.reshape(shape_out).astype(jnp.bfloat16),
        grad_values.reshape(shape_out).astype(jnp.bfloat16),
    )


def shards(hidden, gain, w_first, w_second, lengths, cotangent):
    encoder = lax.axis_index("section") == 0
    states = hidden[0]
    batch_size, length, width = states.shape
    total_rows = batch_size * length
    gains = gain[0]
    wide = states.astype(jnp.float32)
    inverse = lax.rsqrt(jnp.mean(wide * wide, axis=-1, keepdims=True) + EPS)
    unit = wide * inverse
    normed = (unit * gains).astype(jnp.bfloat16)
    normed_rows = normed.reshape(total_rows, width)
    full_first, full_second = (
        lax.all_gather(w_first[0], "dp", axis=0, tiled=True),
        lax.all_gather(w_second[0], "dp", axis=0, tiled=True),
    )
    columns = full_first.shape[1]
    proj_shape = (batch_size, length, columns)
    first_proj = (
        jnp.dot(normed_rows, full_first, preferred_element_type=jnp.float32)
        .astype(jnp.bfloat16)
        .reshape(proj_shape)
    )

    def values_encoder(operand):
        return (
            jnp.dot(normed_rows, full_second, preferred_element_type=jnp.float32)
            .astype(jnp.bfloat16)
            .reshape(proj_shape)
        )

    def values_decoder(operand):
        return jnp.zeros(proj_shape, jnp.bfloat16)

    second_proj = lax.cond(encoder, values_encoder, values_decoder, 0)
    keys, values = passed_along((first_proj, second_proj), "section", 1)
    heads_here = columns // HEAD
    weight_shape = (batch_size, heads_here, length, length)

    def forward_decoder(operand):
        context, weights, weights_low = attend(first_proj, keys, values, lengths[:, 0])
        out_part = contract_last(context.reshape(total_rows, columns), full_second)
        return (context, weights, weights_low, out_part)

    def forward_encoder(operand):
        return (
            jnp.zeros(proj_shape, jnp.bfloat16),
            jnp.zeros(weight_shape, jnp.float32),
            jnp.zeros(weight_shape, jnp.bfloat16),
            jnp.zeros((total_rows, width), jnp.float32),
        )

    context, weights, weights_low, out_part = lax.cond(encoder, forward_encoder, forward_decoder, 0)
    wide_rows = wide.reshape(total_rows, width)
    unit_rows = unit.reshape(total_rows, width)
    inverse_rows = inverse.reshape(total_rows, 1)
    output_rows = (wide_rows + total_features(out_part)).astype(jnp.bfloat16)
    result = jnp.where(encoder, normed, output_rows.reshape(batch_size, length, width))
    target_keep = jnp.arange(length)[None, :] < lengths[:, 1][:, None]
    grad_out = jnp.where(target_keep[:, :, None], cotangent[0], jnp.zeros((), jnp.bfloat16))
    grad_out_rows = grad_out.reshape(total_rows, width)

    def backward_decoder(operand):
        grad_context = (
            jnp.dot(grad_out_rows, full_second, preferred_element_type=jnp.float32)
            .astype(jnp.bfloat16)
            .reshape(proj_shape)
        )
        return attend_back(grad_context, first_proj, keys, values, weights, weights_low)

    def backward_encoder(operand):
        empty = jnp.zeros(proj_shape, jnp.bfloat16)
        return (empty, empty, empty)

    grad_query, grad_key, grad_value = lax.cond(encoder, backward_encoder, backward_decoder, 0)
    back_key, back_value = passed_along((grad_key, grad_value), "section", -1)
    grad_first = jnp.where(encoder, back_key, grad_query).reshape(total_rows, columns)
    grad_second = jnp.where(encoder, back_value, jnp.zeros((), jnp.bfloat16)).reshape(
        total_rows, columns
    )
    second_left = jnp.where(encoder, normed, grad_out).reshape(total_rows, width)
    second_right = jnp.where(encoder, back_value, context).reshape(total_rows, columns)
    weight_first = contract_rows(normed_rows, grad_first)
    weight_second = contract_rows(second_left, second_right)

    def back_encoder(operand):
        return contract_last(grad_first, full_first) + contract_last(grad_second, full_second)

    def back_decoder(operand):
        return contract_last(grad_first, full_first)

    back_part = lax.cond(encoder, back_encoder, back_decoder, 0)
    extra_rows = jnp.where(encoder, cotangent[0].astype(jnp.float32), 0.0).reshape(
        total_rows, width
    )
    residual_rows = jnp.where(encoder, 0.0, grad_out.astype(jnp.float32)).reshape(total_rows, width)
    grad_normed = total_features(back_part) + extra_rows
    scaled = grad_normed * gains
    inner = jnp.mean(scaled * unit_rows, axis=-1, keepdims=True)
    grad_states = (inverse_rows * (scaled - unit_rows * inner) + residual_rows).astype(jnp.bfloat16)
    gain_part = jnp.sum(grad_normed * unit_rows, axis=0)
    first_sum, second_sum, gain_sum = (
        lax.psum_scatter(
            weight_first.astype(jnp.bfloat16), "dp", scatter_dimension=0, tiled=True
        ).astype(jnp.float32),
        lax.psum_scatter(
            weight_second.astype(jnp.bfloat16), "dp", scatter_dimension=0, tiled=True
        ).astype(jnp.float32),
        lax.psum_scatter(
            gain_part.astype(jnp.bfloat16), "dp", scatter_dimension=0, tiled=True
        ).astype(jnp.float32),
    )
    return (
        result[None],
        grad_states.reshape(batch_size, length, width)[None],
        gain_sum[None],
        first_sum[None],
        second_sum[None],
    )


def solution(mesh):
    return jax.shard_map(
        shards,
        mesh=mesh,
        in_specs=(
            P("section", "dp", None, None),
            P("section", None),
            P("section", "dp", "mp"),
            P("section", "dp", "mp"),
            P("dp", None),
            P("section", "dp", None, None),
        ),
        out_specs=(
            P("section", "dp", None, None),
            P("section", "dp", None, None),
            P("section", "dp"),
            P("section", "dp", "mp"),
            P("section", "dp", "mp"),
        ),
        check_vma=False,
    )
```

profile of v0, /device:TPU:0, one launch (start us, length us, event | category | flops | bytes accessed | tf_op | source)
XLA Modules:
  0.0 682.9 jit_solution(3879700864426107040)
XLA Ops:
  7.2 0.0 copy-start
  7.2 0.0 copy-start.10
  7.2 0.0 all-gather.5.cloned.1.call-start
  7.2 0.7 all-gather.5.cloned.1.call-update
  7.9 0.0 all-gather.7.cloned.1.call-start
  8.0 0.7 all-gather.7.cloned.1.call-update
  8.7 0.0 reduce-scatter.3.cloned.1.call-start
  8.7 1.2 slice.6
  10.0 0.6 iota_compare_fusion.1
  10.6 2.3 fusion.36
  13.0 0.0 copy-done
  13.0 3.0 fusion.28
  16.0 62.1 %all-gather.5.cloned.1.call-done = bf16[1,5120,640]{2,1,0:T(8,128)(2,1)} async-done(((bf16[1,320,640]{2,1,0:T(8,128)(2,1)}), bf16[1,5120,640]{2,1,0:T(8,128)(2,1)}) %all-gather.5.cloned.1.call-update) | async-done | bytes 6553616 | tf_op jit(solution)/shard_map/all_gather | solution.py:99
  78.1 0.0 copy-done.10
  78.1 5.1 convolution_convert_fusion.8
  83.2 3.2 collective-permute-start
  86.4 59.0 %all-gather.7.cloned.1.call-done = bf16[1,5120,640]{2,1,0:T(8,128)(2,1)} async-done(((bf16[1,320,640]{2,1,0:T(8,128)(2,1)}), bf16[1,5120,640]{2,1,0:T(8,128)(2,1)}) %all-gather.7.cloned.1.call-update) | async-done | bytes 6553616 | tf_op jit(solution)/shard_map/all_gather | solution.py:100
  145.4 5.9 conditional.4
  145.4 5.9 fusion
  151.3 0.0 copy-start.11
  151.3 0.9 copy.53
  152.2 2.0 collective-permute-start.1
  154.2 3.5 bitcast_select_fusion
  157.7 0.0 collective-permute-done
  157.7 3.8 collective-permute-done.1
  161.5 0.0 copy-done.9
  161.5 4.9 conditional.5
  161.5 1.2 broadcast.147
  162.7 2.9 broadcast.149
  165.6 0.8 broadcast.146.clone
  166.3 1.5 conditional.6
  166.3 0.8 broadcast.151
  167.1 0.8 broadcast.151.clone.1
  167.9 1.2 copy.59
  169.1 1.3 collective-permute-start.2
  170.4 40.9 %collective-permute-done.2 = bf16[1,256,640]{2,1,0:T(8,128)(2,1)S(1)} collective-permute-done((bf16[1,256,640]{2,1,0:T(8,128)(2,1)S(1)}, bf16[1,256,640]{2,1,0:T(8,128)(2,1)S(1)}, u32[]{:S(2)}, u32[]{:S(2)}) %collective-permute-start.2) | collective-permute-done | bytes 327712 | tf_op jit(solution)/shard_map/ppermute | solution.py:15
  211.3 5.1 convolution_convert_fusion.7
  216.4 0.0 reduce-scatter.3.cloned.1.call-update
  216.5 0.0 reduce-scatter.5.cloned.1.call-start
  216.5 0.9 copy-done.8
  217.4 0.9 copy.61
  218.3 1.3 collective-permute-start.3
  219.6 9.6 %collective-permute-done.3 = bf16[1,256,640]{2,1,0:T(8,128)(2,1)S(1)} collective-permute-done((bf16[1,256,640]{2,1,0:T(8,128)(2,1)}, bf16[1,256,640]{2,1,0:T(8,128)(2,1)S(1)}, u32[]{:S(2)}, u32[]{:S(2)}) %collective-permute-start.3) | collective-permute-done | bytes 327712 | tf_op jit(solution)/shard_map/ppermute | solution.py:15
  229.2 7.8 %convolution_convert_fusion.6 = bf16[5120,640]{1,0:T(8,128)(2,1)} fusion(bf16[1,1,256,5120]{3,2,1,0:T(8,128)(2,1)} %param.19, pred[256]{0:T(512)(128)(4,1)S(1)} %iota_compare_fusion.1, pred[]{:T(512)} %eq.3, bf16[1,1,256,5120]{3,2,1,0:T(8,128)(2,1)S(1)} %copy-done, f32[5120]{0:T(1024)S(1)} %bitcast.184, f32[256]{0:T(256)S(1)} %add_rsqrt_fusion, ...), kind=kOutput, calls=%fused_computation.33 | convolution fusion | flops 1689026560 | bytes 12473601 | tf_op jit(solution)/shard_map/dot_general | solution.py:19
  237.0 0.0 reduce-scatter.5.cloned.1.call-update
  237.0 0.0 all-reduce.4.cloned.1.call-start
  237.1 10.2 %conditional.7 = (f32[256,5120]{1,0:T(8,128)}) conditional(s32[]{:T(128)} %convert_element_type.199, (bf16[256,640]{1,0:T(8,128)(2,1)S(1)}, bf16[5120,640]{1,0:T(8,128)(2,1)}) %tuple.78, (bf16[256,640]{1,0:T(8,128)(2,1)S(1)}, bf16[5120,640]{1,0:T(8,128)(2,1)}, pred[]{:T(512)}, bf16[1,256,640]{2,1,0:T(8,128)(2,1)S(1)}, ...), branch_computations={%region_11.12_spmd, %region_12.13_spmd} | conditional | flops 3356917760 | bytes 55705636 | solution.py:177
  237.3 5.3 fusion.59
  242.7 4.6 convolution_add_fusion
  247.3 0.0 all-reduce.4.cloned.1.call-update
  247.3 0.6 copy-done.12
  248.0 0.6 dynamic-slice
  249.2 55.4 %reduce-scatter.3.cloned.1.call-done = bf16[320,640]{1,0:T(8,128)(2,1)} async-done(((bf16[5120,640]{1,0:T(8,128)(2,1)}), bf16[320,640]{1,0:T(8,128)(2,1)}) %reduce-scatter.3.cloned.1.call-update) | async-done | bytes 409616 | tf_op jit(solution)/shard_map/reduce_scatter | solution.py:188
  304.6 1.9 bitcast_convert_fusion.1
  306.6 92.4 %reduce-scatter.5.cloned.1.call-done = bf16[320,640]{1,0:T(8,128)(2,1)} async-done(((bf16[5120,640]{1,0:T(8,128)(2,1)}), bf16[320,640]{1,0:T(8,128)(2,1)}) %reduce-scatter.5.cloned.1.call-update) | async-done | bytes 409616 | tf_op jit(solution)/shard_map/reduce_scatter | solution.py:191
  398.9 1.9 bitcast_convert_fusion
  400.9 194.1 %all-reduce.4.cloned.1.call-done = (f32[256,5120]{1,0:T(8,128)}, f32[256,5120]{1,0:T(8,128)}) async-done(((f32[256,5120]{1,0:T(8,128)}, f32[256,5120]{1,0:T(8,128)}), (f32[256,5120]{1,0:T(8,128)}, f32[256,5120]{1,0:T(8,128)})) %all-reduce.4.cloned.1.call-update) | async-done | bytes 10485776 | tf_op jit(solution)/shard_map/psum | solution.py:31
  595.0 5.3 fusion.40
  600.3 0.0 copy-done.4
  600.3 2.2 fusion.34
  602.5 3.8 fusion.41
  606.4 69.4 %all-reduce = bf16[5120]{0:T(1024)(128)(2,1)S(1)} all-reduce(bf16[5120]{0:T(1024)(128)(2,1)S(1)} %get-tuple-element.131), channel_id=4, replica_groups=mesh['section'=2,'dp'=16,'mp'=4] {'dp'}, use_global_device_ids=true, to_apply=%region_16.17.clone | all-reduce | flops 5120 | bytes 20480
  675.7 0.1 dynamic-slice_convert_fusion
  675.8 0.6 reshape.361
  (14 shorter events, 0.1 us)
Async XLA Ops:
  7.2 5.8 copy-start
  7.2 70.9 %copy-start.10 = (f32[1,5120]{1,0:T(1,128)S(1)}, f32[1,5120]{1,0:T(1,128)}, u32[]{:S(2)}) copy-start(f32[1,5120]{1,0:T(1,128)} %param.15) | copy-start | bytes 61444
  7.2 70.9 %all-gather.5.cloned.1.call-start = ((), (), s32[]{:S(2)}) async-start(), calls=%async_computation.4 | async-start | bytes 6963200 | tf_op jit(solution)/shard_map/all_gather | solution.py:99
  7.9 137.5 %all-gather.7.cloned.1.call-start = ((), (), s32[]{:S(2)}) async-start(), calls=%async_computation.5 | async-start | bytes 6963200 | tf_op jit(solution)/shard_map/all_gather | solution.py:100
  8.7 296.0 %reduce-scatter.3.cloned.1.call-start = ((), (), s32[]{:S(2)}) async-start(), calls=%async_computation.2 | async-start | bytes 6963200 | tf_op jit(solution)/shard_map/reduce_scatter | solution.py:188
  83.2 78.3 %copy-start.9 = (bf16[256,640]{1,0:T(8,128)(2,1)}, bf16[256,640]{1,0:T(8,128)(2,1)S(1)}, u32[]{:S(2)}) copy-start(bf16[256,640]{1,0:T(8,128)(2,1)S(1)} %convolution_convert_fusion.8) | copy-start | bytes 983044
  83.2 74.5 %collective-permute-start = (bf16[1,256,640]{2,1,0:T(8,128)(2,1)S(1)}, bf16[1,256,640]{2,1,0:T(8,128)(2,1)}, u32[]{:S(2)}, u32[]{:S(2)}) collective-permute-start(bf16[1,256,640]{2,1,0:T(8,128)(2,1)S(1)} %bitcast.180), channel_id=1, source_target_pairs={{0,64},{1,65},{2,66},{3,67},{4,68},{5,69},{6,70},{7,71},{8,72},{9,... | collective-permute-start | bytes 983048 | tf_op jit(solution)/shard_map/ppermute | solution.py:15
  151.3 10.2 %copy-start.11 = (s32[1,2]{1,0:T(1,128)S(1)}, s32[1,2]{1,0:T(1,128)}, u32[]{:S(2)}) copy-start(s32[1,2]{1,0:T(1,128)} %param.18) | copy-start | bytes 28
  152.2 9.3 %collective-permute-start.1 = (bf16[1,256,640]{1,2,0:T(8,128)(2,1)}, bf16[1,256,640]{1,2,0:T(8,128)(2,1)}, u32[]{:S(2)}, u32[]{:S(2)}) collective-permute-start(bf16[1,256,640]{1,2,0:T(8,128)(2,1)} %copy.53), channel_id=1, source_target_pairs={{0,64},{1,65},{2,66},{3,67},{4,68},{5,69},{6,70},{7,71},{8,72},{9,... | collective-permute-start | bytes 983048 | tf_op jit(solution)/shard_map/ppermute | solution.py:15
  169.1 42.2 %collective-permute-start.2 = (bf16[1,256,640]{2,1,0:T(8,128)(2,1)S(1)}, bf16[1,256,640]{2,1,0:T(8,128)(2,1)S(1)}, u32[]{:S(2)}, u32[]{:S(2)}) collective-permute-start(bf16[1,256,640]{2,1,0:T(8,128)(2,1)S(1)} %copy.59), channel_id=1, source_target_pairs={{64,0},{65,1},{66,2},{67,3},{68,4},{69,5},{70,6},{71,7},{72,8},{73... | collective-permute-start | bytes 983048 | tf_op jit(solution)/shard_map/ppermute | solution.py:15
  216.4 1.0 copy-start.8
  216.5 182.5 %reduce-scatter.5.cloned.1.call-start = ((), (), s32[]{:S(2)}) async-start(), calls=%async_computation.3 | async-start | bytes 6963200 | tf_op jit(solution)/shard_map/reduce_scatter | solution.py:191
  218.3 10.9 %collective-permute-start.3 = (bf16[1,256,640]{2,1,0:T(8,128)(2,1)}, bf16[1,256,640]{2,1,0:T(8,128)(2,1)S(1)}, u32[]{:S(2)}, u32[]{:S(2)}) collective-permute-start(bf16[1,256,640]{2,1,0:T(8,128)(2,1)} %copy.61), channel_id=1, source_target_pairs={{64,0},{65,1},{66,2},{67,3},{68,4},{69,5},{70,6},{71,7},{72,8},{73... | collective-permute-start | bytes 983048 | tf_op jit(solution)/shard_map/ppermute | solution.py:15
  237.0 358.0 %all-reduce.4.cloned.1.call-start = ((), (), s32[]{:S(2)}) async-start(), calls=%async_computation.6 | async-start | bytes 20971520 | tf_op jit(solution)/shard_map/psum | solution.py:31
  237.3 5.4 copy-start.2
  247.3 0.7 copy-start.12
  595.0 5.3 copy-start.3
  595.0 5.3 copy-start.4
Sparse Core Ops, SparseCore 0:
  10.5 67.5 all-gather.4
  80.5 64.8 all-gather.6
  216.6 88.0 reduce-scatter.2
  309.3 89.6 reduce-scatter.4
  401.4 193.5 all-reduce.3
where the time goes:
time: 684 us; the launch traced here: 683 us
  waiting for transfers between devices  519 us (76%)
  blocking collectives  69.4 us (10%)
  matrix products  33.8 us (5%)
  other arithmetic  24.8 us (4%)
  between operations  14.5 us (2%)
  local copies, waits for them, and re-layouts  13.3 us (2%)
  starting transfers between devices  8.01 us (1%)
    psum x1, waiting for transfers between devices, total_features(): return lax.psum(partial_value, 'mp')  194 us
    reduce_scatter x1, waiting for transfers between devices, shards(): lax.psum_scatter(weight_second.astype(jnp.bfloat16), 'dp', scatter_dimens...  92.4 us
    unnamed x1, blocking collectives  69.4 us
    all_gather x1, waiting for transfers between devices, shards(): lax.all_gather(w_first[0], 'dp', axis=0, tiled=True)  62.1 us
    all_gather x1, waiting for transfers between devices, shards(): lax.all_gather(w_second[0], 'dp', axis=0, tiled=True)  59 us
    reduce_scatter x1, waiting for transfers between devices, shards(): lax.psum_scatter(weight_first.astype(jnp.bfloat16), 'dp', scatter_dimensi...  55.4 us
    ppermute x4, waiting for transfers between devices, passed_along(): return lax.ppermute(shard, axis, pairs)  54.3 us
  transfers between devices with their start and end apart: 9, of which 8 were waited for; matrix products, arithmetic and copies ran while one was open for 7% of the time, Pallas kernels for 0%

commit v1 on v0

--- a/solution.py
+++ b/solution.py
@@ -28,7 +28,12 @@
 
 
 def total_features(partial_value):
-    return lax.psum(partial_value, "mp")
+
+    def derive_meshes_now(inputs):
+        wide_out = lax.all_gather(inputs, axis_name="mp").sum(axis=0)
+        return wide_out
+
+    return derive_meshes_now(partial_value)
 
 
 def split_heads(values_in):

time: 684 us -> 886 us (1.30)
  waiting for transfers between devices: 519 us -> 697 us
  other arithmetic: 24.8 us -> 47.9 us
    all_gather x0 -> x2, waiting for transfers between devices: none -> 362 us  [derive_meshes_now(): wide_out = lax.all_gather(inputs, axis_name='mp').sum(axis=0)]
    psum x1 -> x0, waiting for transfers between devices: 194 us -> none  [total_features(): return lax.psum(partial_value, 'mp')]
    reduce_scatter x1, waiting for transfers between devices: 55.4 us -> 92.4 us  [shards(): lax.psum_scatter(weight_first.astype(jnp.bfloat16), 'dp', scatter_dimensi...]
    reduce_scatter x1, waiting for transfers between devices: 92.4 us -> 59.7 us  [shards(): lax.psum_scatter(weight_second.astype(jnp.bfloat16), 'dp', scatter_dimens...]
    reduce_sum x0 -> x2, other arithmetic: none -> 22.3 us  [derive_meshes_now(): wide_out = lax.all_gather(inputs, axis_name='mp').sum(axis=0)]
  transfers between devices with their start and end apart: 9 -> 10, of which waited for: 8 -> 9; matrix products, arithmetic and copies ran while one was open for 7% -> 7% of each run, Pallas kernels for 0% -> 0%
where the time goes in v1:
time: 886 us; the launch traced here: 885 us
  waiting for transfers between devices  697 us (79%)
  blocking collectives  69.4 us (8%)
  other arithmetic  47.9 us (5%)
  matrix products  34.8 us (4%)
  between operations  14.9 us (2%)
  local copies, waits for them, and re-layouts  13.1 us (1%)
    all_gather x2, waiting for transfers between devices, derive_meshes_now(): wide_out = lax.all_gather(inputs, axis_name='mp').sum(axis=0)  362 us
    reduce_scatter x1, waiting for transfers between devices, shards(): lax.psum_scatter(weight_first.astype(jnp.bfloat16), 'dp', scatter_dimensi...  92.4 us
    unnamed x1, blocking collectives  69.4 us
    all_gather x1, waiting for transfers between devices, shards(): lax.all_gather(w_second[0], 'dp', axis=0, tiled=True)  64 us
    reduce_scatter x1, waiting for transfers between devices, shards(): lax.psum_scatter(weight_second.astype(jnp.bfloat16), 'dp', scatter_dimens...  59.7 us
    all_gather x1, waiting for transfers between devices, shards(): lax.all_gather(w_first[0], 'dp', axis=0, tiled=True)  59.1 us
    ppermute x4, waiting for transfers between devices, passed_along(): return lax.ppermute(shard, axis, pairs)  57.1 us
    reduce_sum x2, other arithmetic, derive_meshes_now(): wide_out = lax.all_gather(inputs, axis_name='mp').sum(axis=0)  22.3 us
  transfers between devices with their start and end apart: 10, of which 9 were waited for; matrix products, arithmetic and copies ran while one was open for 7% of the time, Pallas kernels for 0%

profile of v1, /device:TPU:0, one launch (start us, length us, event | category | flops | bytes accessed | tf_op | source)
XLA Modules:
  0.0 884.7 jit_solution(15287927350816567501)
XLA Ops:
  7.2 0.0 all-gather.11.cloned.1.call-start
  7.2 0.7 all-gather.11.cloned.1.call-update
  7.9 0.0 all-gather.9.cloned.1.call-start
  8.0 0.7 all-gather.9.cloned.1.call-update
  8.7 0.0 reduce-scatter.5.cloned.1.call-start
  8.7 2.3 fusion.37
  11.1 3.0 fusion.43
  14.1 64.0 %all-gather.11.cloned.1.call-done = bf16[1,5120,640]{2,1,0:T(8,128)(2,1)} async-done(((bf16[1,320,640]{2,1,0:T(8,128)(2,1)}), bf16[1,5120,640]{2,1,0:T(8,128)(2,1)}) %all-gather.11.cloned.1.call-update) | async-done | bytes 6553616 | tf_op jit(solution)/shard_map/all_gather | solution.py:105
  78.1 5.9 conditional.4
  78.1 5.9 fusion
  83.9 0.9 copy.53
  84.8 2.2 collective-permute-start.1
  87.0 59.1 %all-gather.9.cloned.1.call-done = bf16[1,5120,640]{2,1,0:T(8,128)(2,1)} async-done(((bf16[1,320,640]{2,1,0:T(8,128)(2,1)}), bf16[1,5120,640]{2,1,0:T(8,128)(2,1)}) %all-gather.9.cloned.1.call-update) | async-done | bytes 6553616 | tf_op jit(solution)/shard_map/all_gather | solution.py:104
  146.1 5.9 convolution_convert_fusion.7
  151.9 3.2 collective-permute-start
  155.2 0.6 slice.6
  155.7 0.6 iota_compare_fusion.1
  156.4 0.0 collective-permute-done.1
  156.4 5.4 collective-permute-done
  161.8 5.8 conditional.5
  161.8 3.0 broadcast.183
  164.8 1.2 broadcast.181
  166.0 0.9 broadcast.182
  166.9 0.8 broadcast.180.clone
  167.6 1.5 conditional.6
  167.6 0.7 broadcast.185
  168.4 0.8 broadcast.185.clone
  169.2 0.2 copy.61
  169.4 1.3 collective-permute-start.3
  170.7 42.7 %collective-permute-done.3 = bf16[1,256,640]{2,1,0:T(8,128)(2,1)S(1)} collective-permute-done((bf16[1,256,640]{2,1,0:T(8,128)(2,1)S(1)}, bf16[1,256,640]{2,1,0:T(8,128)(2,1)S(1)}, u32[]{:S(2)}, u32[]{:S(2)}) %collective-permute-start.3) | collective-permute-done | bytes 327712 | tf_op jit(solution)/shard_map/ppermute | solution.py:15
  213.4 0.7 copy-done.8
  214.1 7.6 convolution_convert_fusion.5
  221.7 0.0 reduce-scatter.5.cloned.1.call-update
  221.7 0.0 reduce-scatter.3.cloned.1.call-start
  221.8 1.2 copy.59
  223.0 1.3 collective-permute-start.2
  224.3 9.0 %collective-permute-done.2 = bf16[1,256,640]{2,1,0:T(8,128)(2,1)S(1)} collective-permute-done((bf16[1,256,640]{2,1,0:T(8,128)(2,1)S(1)}, bf16[1,256,640]{2,1,0:T(8,128)(2,1)S(1)}, u32[]{:S(2)}, u32[]{:S(2)}) %collective-permute-start.2) | collective-permute-done | bytes 327712 | tf_op jit(solution)/shard_map/ppermute | solution.py:15
  233.3 5.2 convolution_convert_fusion.6
  238.5 0.0 reduce-scatter.3.cloned.1.call-update
  238.6 0.0 all-gather.13.cloned.1.call-start
  238.6 0.5 all-gather.13.cloned.1.call-update
  239.2 0.0 all-gather.15.cloned.1.call-start
  239.2 0.3 copy-done.9
  239.5 10.3 %conditional.7 = (f32[256,5120]{1,0:T(8,128)}) conditional(s32[]{:T(128)} %convert_element_type.211, (bf16[256,640]{1,0:T(8,128)(2,1)S(1)}, bf16[5120,640]{1,0:T(8,128)(2,1)}) %tuple.79, (bf16[256,640]{1,0:T(8,128)(2,1)S(1)}, bf16[5120,640]{1,0:T(8,128)(2,1)}, pred[]{:T(512)}, bf16[1,256,640]{2,1,0:T(8,128)(2,1)S(1)}, ...), branch_computations={%region_11.12_spmd, %region_12.13_spmd} | conditional | flops 3356917760 | bytes 55705636 | solution.py:182
  239.5 5.7 fusion.64
  245.3 4.5 convolution_add_fusion
  249.8 0.0 all-gather.15.cloned.1.call-update
  249.8 0.6 copy-done.11
  250.5 0.6 dynamic-slice
  251.7 59.7 %reduce-scatter.5.cloned.1.call-done = bf16[320,640]{1,0:T(8,128)(2,1)} async-done(((bf16[5120,640]{1,0:T(8,128)(2,1)}), bf16[320,640]{1,0:T(8,128)(2,1)}) %reduce-scatter.5.cloned.1.call-update) | async-done | bytes 409616 | tf_op jit(solution)/shard_map/reduce_scatter | solution.py:196
  311.4 1.9 bitcast_convert_fusion
  313.3 92.4 %reduce-scatter.3.cloned.1.call-done = bf16[320,640]{1,0:T(8,128)(2,1)} async-done(((bf16[5120,640]{1,0:T(8,128)(2,1)}), bf16[320,640]{1,0:T(8,128)(2,1)}) %reduce-scatter.3.cloned.1.call-update) | async-done | bytes 409616 | tf_op jit(solution)/shard_map/reduce_scatter | solution.py:193
  405.7 1.9 bitcast_convert_fusion.1
  407.6 188.3 %all-gather.13.cloned.1.call-done = f32[1024,5120]{1,0:T(8,128)} async-done(((f32[256,5120]{1,0:T(8,128)}), f32[1024,5120]{1,0:T(8,128)}) %all-gather.13.cloned.1.call-update) | async-done | bytes 20971536 | tf_op jit(solution)/shard_map/all_gather | solution.py:33
  595.9 11.2 %reduce_sum.68 = f32[256,5120]{1,0:T(8,128)} reduce(f32[4,256,5120]{2,1,0:T(8,128)} %bitcast.148, f32[]{:T(128)} %constant.23.clone.1), dimensions={0}, to_apply=%region_7.8 | reduce | flops 3932160 | bytes 26214404 | tf_op jit(solution)/shard_map/reduce_sum | solution.py:33
  607.1 6.2 fusion.47
  613.3 174.0 %all-gather.15.cloned.1.call-done = f32[1024,5120]{1,0:T(8,128)} async-done(((f32[256,5120]{1,0:T(8,128)}), f32[1024,5120]{1,0:T(8,128)}) %all-gather.15.cloned.1.call-update) | async-done | bytes 20971536 | tf_op jit(solution)/shard_map/all_gather | solution.py:33
  787.4 11.1 %reduce_sum.70 = f32[256,5120]{1,0:T(8,128)} reduce(f32[4,256,5120]{2,1,0:T(8,128)} %bitcast.149, f32[]{:T(128)} %constant.23.clone.1), dimensions={0}, to_apply=%region_13.14 | reduce | flops 3932160 | bytes 26214404 | tf_op jit(solution)/shard_map/reduce_sum | solution.py:33
  798.4 5.5 fusion.45
  804.0 0.0 copy-done.3
  804.0 3.8 fusion.36
  807.9 69.4 %all-reduce = bf16[5120]{0:T(1024)(128)(2,1)S(1)} all-reduce(bf16[5120]{0:T(1024)(128)(2,1)S(1)} %get-tuple-element.141), channel_id=6, replica_groups=mesh['section'=2,'dp'=16,'mp'=4] {'dp'}, use_global_device_ids=true, to_apply=%region_16.17.clone | all-reduce | flops 5120 | bytes 20480
  877.2 0.1 dynamic-slice_convert_fusion
  877.3 0.6 reshape.411
  (20 shorter events, 0.1 us)
Async XLA Ops:
  7.2 3.9 copy-start
  7.2 70.9 %all-gather.11.cloned.1.call-start = ((), (), s32[]{:S(2)}) async-start(), calls=%async_computation.5 | async-start | bytes 6963200 | tf_op jit(solution)/shard_map/all_gather | solution.py:105
  7.9 138.2 %all-gather.9.cloned.1.call-start = ((), (), s32[]{:S(2)}) async-start(), calls=%async_computation.4 | async-start | bytes 6963200 | tf_op jit(solution)/shard_map/all_gather | solution.py:104
  8.7 302.7 %reduce-scatter.5.cloned.1.call-start = ((), (), s32[]{:S(2)}) async-start(), calls=%async_computation.3 | async-start | bytes 6963200 | tf_op jit(solution)/shard_map/reduce_scatter | solution.py:196
  84.8 70.3 %copy-start.10 = (s32[1,2]{1,0:T(1,128)S(1)}, s32[1,2]{1,0:T(1,128)}, u32[]{:S(2)}) copy-start(s32[1,2]{1,0:T(1,128)} %param.18) | copy-start | bytes 28
  84.8 71.6 %collective-permute-start.1 = (bf16[1,256,640]{1,2,0:T(8,128)(2,1)}, bf16[1,256,640]{1,2,0:T(8,128)(2,1)}, u32[]{:S(2)}, u32[]{:S(2)}) collective-permute-start(bf16[1,256,640]{1,2,0:T(8,128)(2,1)} %copy.53), channel_id=1, source_target_pairs={{0,64},{1,65},{2,66},{3,67},{4,68},{5,69},{6,70},{7,71},{8,72},{9,... | collective-permute-start | bytes 983048 | tf_op jit(solution)/shard_map/ppermute | solution.py:15
  151.9 9.9 %collective-permute-start = (bf16[1,256,640]{2,1,0:T(8,128)(2,1)S(1)}, bf16[1,256,640]{2,1,0:T(8,128)(2,1)}, u32[]{:S(2)}, u32[]{:S(2)}) collective-permute-start(bf16[1,256,640]{2,1,0:T(8,128)(2,1)S(1)} %bitcast.159), channel_id=1, source_target_pairs={{0,64},{1,65},{2,66},{3,67},{4,68},{5,69},{6,70},{7,71},{8,72},{9,... | collective-permute-start | bytes 983048 | tf_op jit(solution)/shard_map/ppermute | solution.py:15
  167.6 46.5 %copy-start.7 = (f32[1,5120]{1,0:T(1,128)S(1)}, f32[1,5120]{1,0:T(1,128)}, u32[]{:S(2)}) copy-start(f32[1,5120]{1,0:T(1,128)} %param.15) | copy-start | bytes 61444
  169.4 44.0 %collective-permute-start.3 = (bf16[1,256,640]{2,1,0:T(8,128)(2,1)S(1)}, bf16[1,256,640]{2,1,0:T(8,128)(2,1)S(1)}, u32[]{:S(2)}, u32[]{:S(2)}) collective-permute-start(bf16[1,256,640]{2,1,0:T(8,128)(2,1)S(1)} %copy.61), channel_id=1, source_target_pairs={{64,0},{65,1},{66,2},{67,3},{68,4},{69,5},{70,6},{71,7},{72,8},{73... | collective-permute-start | bytes 983048 | tf_op jit(solution)/shard_map/ppermute | solution.py:15
  213.4 0.7 copy-start.8
  221.7 11.6 %copy-start.5 = (bf16[1,256,640]{2,1,0:T(8,128)(2,1)S(1)}, bf16[1,256,640]{2,1,0:T(8,128)(2,1)}, u32[]{:S(2)}) copy-start(bf16[1,256,640]{2,1,0:T(8,128)(2,1)} %get-tuple-element.140) | copy-start | bytes 983044
  221.7 184.0 %reduce-scatter.3.cloned.1.call-start = ((), (), s32[]{:S(2)}) async-start(), calls=%async_computation.2 | async-start | bytes 6963200 | tf_op jit(solution)/shard_map/reduce_scatter | solution.py:193
  223.0 10.3 %collective-permute-start.2 = (bf16[1,256,640]{2,1,0:T(8,128)(2,1)S(1)}, bf16[1,256,640]{2,1,0:T(8,128)(2,1)S(1)}, u32[]{:S(2)}, u32[]{:S(2)}) collective-permute-start(bf16[1,256,640]{2,1,0:T(8,128)(2,1)S(1)} %copy.59), channel_id=1, source_target_pairs={{64,0},{65,1},{66,2},{67,3},{68,4},{69,5},{70,6},{71,7},{72,8},{73... | collective-permute-start | bytes 983048 | tf_op jit(solution)/shard_map/ppermute | solution.py:15
  238.5 1.0 copy-start.9
  238.6 357.3 %all-gather.13.cloned.1.call-start = ((), (), s32[]{:S(2)}) async-start(), calls=%async_computation.6 | async-start | bytes 26214400 | tf_op jit(solution)/shard_map/all_gather | solution.py:33
  239.2 548.2 %all-gather.15.cloned.1.call-start = ((), (), s32[]{:S(2)}) async-start(), calls=%async_computation.7 | async-start | bytes 26214400 | tf_op jit(solution)/shard_map/all_gather | solution.py:33
  239.5 5.7 copy-start.2
  249.8 0.7 copy-start.11
  798.4 5.6 copy-start.1
  798.4 5.6 copy-start.3
Sparse Core Ops, SparseCore 0:
  10.5 67.5 all-gather.10
  80.5 65.5 all-gather.8
  221.8 89.5 reduce-scatter.4
  316.0 89.6 reduce-scatter.2
  407.2 188.6 all-gather.12
  597.4 189.9 all-gather.14
